TPU v7x, 128 devices: a whole 4x4x4 slice. The times are simulated.
128 devices in a mesh: seq: 16 (over x, y), head: 8 (over z, core).
Axes of the slice: x: 4, y: 4, z: 4, core: 2. Of those that a mesh axis runs over, the one named last changes fastest.
Arguments:
- queries: bfloat16 [32768, 8192], P('seq', 'head'), may hold values from -6 to 6
- key_vectors: bfloat16 [32768, 8192], P('seq', 'head'), may hold values from -6 to 6
- value_vectors: bfloat16 [32768, 8192], P('seq', 'head'), may hold values from -6 to 6
- level_weights: float32 [64, 16, 32768], P('head', None, 'seq'), may hold values from 0.22 to 13.45, as said below
- norm_gain: float32 [8192], P('head'), may hold values from 0.25 to 1.75
Outputs:
- normed: bfloat16 [32768, 8192], P('seq', 'head')
Inputs may be any that keep to these rules, and one draw needn't show every extreme that they name: `level_weights`: positive.
All inputs are finite; a program needn't handle non-finite values.
Results may differ from a plain program's by a relative error of at most 0.0056.
Values may be sent and summed in bfloat16 or wider, within the bound.
A program may use at most 192 MiB of HBM per device.

v0:
```python
import functools

import jax
import jax.numpy as jnp
from jax import lax
from jax.experimental import pallas as pl
from jax.experimental.pallas import tpu as pltpu
from jax.sharding import PartitionSpec as P

D = 128
E = 128
C = 256
HALF = 128
HEADS = 64
MESH = pl.DeviceIdType.MESH
F32 = jnp.float32
BF16 = jnp.bfloat16


def nt(a, b):
    return lax.dot_general(a, b, (((1,), (1,)), ((), ())), preferred_element_type=F32)


def nn(a, b):
    return lax.dot_general(a, b, (((1,), (0,)), ((), ())), preferred_element_type=F32)


def partner_mask(bit):
    return 1 << bit if bit % 2 == 0 else 3 << (bit - 1)


def buckets_of(chunks):
    table = {}
    bit = 0
    while 1 << bit < chunks:
        for start in range(0, chunks, 2 << bit):
            table[(bit, start)] = len(table)
        bit += 1
    return table


def kernel(
    seq_n, head_n, heads, tokens,
    q_hbm, k_hbm, v_hbm, lam_hbm, gain_ref,
    out_ref,
    q_s, k_s, v_s, lam_s, vt_s, acc_s, lv_s, p_s, send_s, recv_s, sq_s, sqx_s, gcol_s, d_s, g_s,
    load_sem, lam_sem, send_sem, recv_sem, sq_send_sem, sq_recv_sem,
):
    chunks = tokens // C
    bits = seq_n.bit_length() - 1
    local_bits = tokens.bit_length() - 1
    me_seq = lax.axis_index("seq")
    me_head = lax.axis_index("head")
    table = buckets_of(chunks)
    scaling = D ** (-0.5)

    def load(which, h):
        src, dst = ((q_hbm, q_s), (k_hbm, k_s), (v_hbm, v_s))[which]
        cols = pl.ds(pl.multiple_of(h * D, D), D)
        return pltpu.make_async_copy(src.at[:, cols], dst.at[h], load_sem.at[which, h])

    lam_copy = pltpu.make_async_copy(lam_hbm, lam_s, lam_sem)

    barrier = pltpu.get_barrier_semaphore()
    for b in range(bits):
        pl.semaphore_signal(
            barrier, inc=1, device_id={"seq": me_seq ^ partner_mask(b)}, device_id_type=MESH
        )
    for k in range(1, head_n):
        pl.semaphore_signal(
            barrier, inc=1, device_id={"head": lax.rem(me_head + k, head_n)}, device_id_type=MESH
        )

    for h in range(heads):
        load(2, h).start()
        load(1, h).start()
    lam_copy.start()

    def state_copy(b, h):
        return pltpu.make_async_remote_copy(
            src_ref=send_s.at[b, h],
            dst_ref=recv_s.at[h, b],
            send_sem=send_sem.at[b, h],
            recv_sem=recv_sem.at[b, h],
            device_id={"seq": me_seq ^ partner_mask(b)},
            device_id_type=MESH,
        )

    for h in range(heads):
        row = jnp.broadcast_to(gain_ref[h : h + 1, :], (E, E))
        gcol_s[h] = row.T

    def states(h):
        load(2, h).wait()
        load(1, h).wait()
        load(0, h).start()
        parts = []
        for c in range(chunks):
            rows = pl.ds(c * C, C)
            vt = v_s[h, rows, :].T
            vt_s[h, :, pl.ds(c * C, C)] = vt
            parts.append(nn(vt, k_s[h, rows, :]))
        size = 1
        bit = 0
        while size < chunks:
            for start in range(0, chunks, 2 * size):
                lv_s[h, table[(bit, start)]] = parts[start // size].astype(BF16)
            parts = [parts[2 * i] + parts[2 * i + 1] for i in range(len(parts) // 2)]
            size *= 2
            bit += 1
        total = parts[0].astype(BF16)
        send_s[0, h] = total
        p_s[h] = total.astype(F32)

    states(0)
    pl.semaphore_wait(barrier, bits + head_n - 1)
    state_copy(0, 0).start()

    @pl.loop(1, heads)
    def _(h):
        states(h)
        state_copy(0, h).start()

    lam_copy.wait()
    for h in range(heads):
        lam_s[h] = lam_s[h] * scaling

    lane = lax.broadcasted_iota(jnp.int32, (8, HALF), 1)
    sub = lax.broadcasted_iota(jnp.int32, (8, HALF), 0)
    low = lane & 7
    low_x = low ^ sub
    low_ok = sub <= low
    high = lane >> 3

    def factors(h, start):
        def row(level):
            return lam_s[h, pl.ds(level, 1), pl.ds(start, HALF)]

        def wide(level):
            return jnp.broadcast_to(row(level), (8, HALF))

        fine = jnp.where(low_x < 2, wide(1), jnp.where(low_x < 4, wide(2), wide(3)))
        fine = jnp.where(low_x == 0, wide(0), fine)
        fine = jnp.where(low_ok, fine, 0.0)
        l4, l5, l6, l7 = wide(4), wide(5), wide(6), wide(7)
        pieces = []
        for half in range(2):
            a = sub + 8 * half
            x = a ^ high
            coarse = jnp.where(x < 2, l4, jnp.where(x < 4, l5, jnp.where(x < 8, l6, l7)))
            coarse = jnp.where(a < high, coarse, 0.0)
            for r in range(8):
                spread = jnp.broadcast_to(coarse[r : r + 1, :], (8, HALF))
                pieces.append(jnp.where(high == 8 * half + r, fine, spread))
        return jnp.concatenate(pieces, axis=0)

    def inside(h):
        load(0, h).wait()
        for c in range(chunks):
            rows = pl.ds(c * C, C)
            q = q_s[h, rows, :]
            lhs = [k_s[h, rows, :]]
            levels = []
            for bit in range(chunks.bit_length() - 1):
                if c >> bit & 1:
                    start = (c >> bit ^ 1) << bit
                    lhs.append(lv_s[h, table[(bit, start)]])
                    levels.append(9 + bit)
            prod = nt(jnp.concatenate(lhs, axis=0), q)
            f0 = factors(h, c * C)
            f1 = factors(h, c * C + HALF)
            l8 = lam_s[h, pl.ds(8, 1), pl.ds(c * C + HALF, HALF)]
            top = jnp.concatenate(
                [(prod[:HALF, :HALF] * f0).astype(BF16), (prod[:HALF, HALF:] * l8).astype(BF16)],
                axis=1,
            )
            bottom = jnp.concatenate(
                [jnp.zeros((HALF, HALF), BF16), (prod[HALF:C, HALF:] * f1).astype(BF16)], axis=1
            )
            weighted = jnp.concatenate([top, bottom], axis=0)
            acc = nn(vt_s[h, :, rows], weighted)
            for i, level in enumerate(levels):
                weight = lam_s[h, pl.ds(level, 1), rows]
                acc = acc + prod[C + i * E : C + (i + 1) * E] * weight
            acc_s[h, :, rows] = acc

    def relay(b, h):
        copy = state_copy(b, h)
        copy.wait_recv()
        if b + 1 < bits:
            total = p_s[h] + recv_s[h, b].astype(F32)
            p_s[h] = total
            send_s[b + 1, h] = total.astype(BF16)
            state_copy(b + 1, h).start()

    LAG = 2

    def relays(slot):
        for b in range(bits):
            h = slot - b * LAG

            @pl.when(jnp.logical_and(h >= 0, h < heads))
            def _():
                relay(b, h)

    sq_s[...] = jnp.zeros_like(sq_s)

    @pl.loop(0, heads)
    def _(h):
        relays(h)
        inside(h)

    on = [(lax.shift_right_logical(me_seq, b) & 1).astype(F32) for b in range(bits)]

    def across(h):
        pieces = 2
        step = E // pieces
        for c in range(chunks):
            rows = pl.ds(c * C, C)
            q = q_s[h, rows, :]
            weights = [lam_s[h, pl.ds(local_bits + 1 + b, 1), rows] * on[b] for b in range(bits)]
            square = sq_s[:, rows]
            lhs = [
                recv_s[h, b, pl.ds(p * step, step), :] for p in range(pieces) for b in range(bits)
            ]
            prod = nt(jnp.concatenate(lhs, axis=0), q)
            for p in range(pieces):
                acc = acc_s[h, pl.ds(p * step, step), rows]
                for b in range(bits):
                    at = (p * bits + b) * step
                    acc = acc + prod[at : at + step] * weights[b]
                acc_s[h, pl.ds(p * step, step), rows] = acc
                sq = acc * acc
                for r in range(step // 8):
                    square = square + sq[r * 8 : (r + 1) * 8]
            sq_s[:, rows] = square

    @pl.loop(0, heads)
    def _(h):
        slot = h + heads
        relays(slot)

        @pl.when(h >= (bits - 1) * LAG)
        def _():
            across(h - (bits - 1) * LAG)

    first = heads - (bits - 1) * LAG

    @pl.loop(max(first, 0), heads)
    def _(h):
        relays(h + heads + (bits - 1) * LAG)
        across(h)

    sqx_s[me_head] = jnp.sum(sq_s[...], axis=0, keepdims=True)

    def sq_copy(k):
        return pltpu.make_async_remote_copy(
            src_ref=sqx_s.at[me_head],
            dst_ref=sqx_s.at[me_head],
            send_sem=sq_send_sem.at[k],
            recv_sem=sq_recv_sem.at[k],
            device_id={"head": lax.rem(me_head + k, head_n)},
            device_id_type=MESH,
        )

    def sq_arrive(k):
        owner = lax.rem(me_head + head_n - k, head_n)
        return pltpu.make_async_remote_copy(
            src_ref=sqx_s.at[owner],
            dst_ref=sqx_s.at[owner],
            send_sem=sq_send_sem.at[k],
            recv_sem=sq_recv_sem.at[k],
            device_id={"head": lax.rem(me_head + k, head_n)},
            device_id_type=MESH,
        )

    for k in range(1, head_n):
        sq_copy(k).start()
    for k in range(1, head_n):
        sq_arrive(k).wait_recv()
    total = sqx_s[0]
    for k in range(1, head_n):
        total = total + sqx_s[k]
    scale = lax.rsqrt(total / (HEADS * E) + 1e-05)
    sqx_s[head_n] = scale

    @pl.loop(0, heads)
    def _(h):
        cols = pl.ds(pl.multiple_of(h * E, E), E)
        for c in range(tokens // HALF):
            rows = pl.ds(c * HALF, HALF)
            value = acc_s[h, :, rows] * gcol_s[h] * sqx_s[head_n, :, rows]
            out_ref[rows, cols] = value.astype(BF16).T

    for b in range(bits):
        for h in range(heads):
            state_copy(b, h).wait_send()
    for k in range(1, head_n):
        sq_copy(k).wait_send()


def body(queries, key_vectors, value_vectors, level_weights, norm_gain):
    tokens = queries.shape[0]
    heads, levels = level_weights.shape[:2]
    seq_n = lax.axis_size("seq")
    head_n = lax.axis_size("head")
    bits = seq_n.bit_length() - 1
    slots = max(len(buckets_of(tokens // C)), 1)
    any_spec = pl.BlockSpec(memory_space=pl.ANY)
    vmem = pl.BlockSpec(memory_space=pltpu.VMEM)
    return pl.pallas_call(
        functools.partial(kernel, seq_n, head_n, heads, tokens),
        out_shape=jax.ShapeDtypeStruct((tokens, heads * E), BF16),
        in_specs=[any_spec] * 4 + [vmem],
        out_specs=vmem,
        scratch_shapes=[
            pltpu.VMEM((heads, tokens, D), BF16),
            pltpu.VMEM((heads, tokens, D), BF16),
            pltpu.VMEM((heads, tokens, E), BF16),
            pltpu.VMEM((heads, levels, tokens), F32),
            pltpu.VMEM((heads, E, tokens), BF16),
            pltpu.VMEM((heads, E, tokens), F32),
            pltpu.VMEM((heads, slots, E, D), BF16),
            pltpu.VMEM((heads, E, D), F32),
            pltpu.VMEM((bits, heads, E, D), BF16),
            pltpu.VMEM((heads, bits, E, D), BF16),
            pltpu.VMEM((8, tokens), F32),
            pltpu.VMEM((head_n + 1, 1, tokens), F32),
            pltpu.VMEM((heads, E, E), F32),
            pltpu.VMEM((8, HALF), F32),
            pltpu.VMEM((16, HALF), F32),
            pltpu.SemaphoreType.DMA((3, heads)),
            pltpu.SemaphoreType.DMA,
            pltpu.SemaphoreType.DMA((bits, heads)),
            pltpu.SemaphoreType.DMA((bits, heads)),
            pltpu.SemaphoreType.DMA((head_n,)),
            pltpu.SemaphoreType.DMA((head_n,)),
        ],
        compiler_params=pltpu.CompilerParams(
            collective_id=0, has_side_effects=True, vmem_limit_bytes=60 * 1024 * 1024
        ),
        name="fenwick",
    )(queries, key_vectors, value_vectors, level_weights, norm_gain.reshape(heads, E))


def solution(mesh):
    placed = (
        P("seq", "head"),
        P("seq", "head"),
        P("seq", "head"),
        P("head", None, "seq"),
        P("head"),
    )
    return jax.shard_map(
        body, mesh=mesh, in_specs=placed, out_specs=P("seq", "head"), check_vma=False
    )
```

profile of v0, /device:TPU:1, one launch (start us, length us, event | category | flops | bytes accessed | tf_op | source)
XLA Modules:
  0.0 52.6 jit_solution(14459176368682360871)
XLA Ops:
  0.0 48.0 %fenwick.1 = bf16[2048,1024]{1,0:T(8,128)(2,1)} custom-call(bf16[2048,1024]{1,0:T(8,128)(2,1)} %q_hbm.1, bf16[2048,1024]{1,0:T(8,128)(2,1)} %k_hbm.1, bf16[2048,1024]{1,0:T(8,128)(2,1)} %v_hbm.1, f32[8,16,2048]{2,1,0:T(8,128)} %lam_hbm.1, f32[8,128]{1,0:T(8,128)} %bitcast.1), custom_call_target="tpu_custom_call" | custom-call | tf_op jit(solution)/shard_map/fenwick/pallas_call | solution.py:311
  48.0 4.6 %copy.7 = bf16[2048,1024]{1,0:T(8,128)(2,1)} copy(bf16[2048,1024]{1,0:T(8,128)(2,1)} %fenwick.1) | data formatting | bytes 8388608
where the time goes:
time: 52.8 us; the launch traced here: 52.6 us
  Pallas kernels  48 us (91%)
  local copies, waits for them, and re-layouts  4.64 us (9%)
    pallas_call x1, Pallas kernels, body(): pl.pallas_call(functools.partial(kernel, seq_n, head_n, heads, tokens), o...  48 us
    unnamed x1, local copies, waits for them, and re-layouts  4.64 us

commit v1 on v0

--- a/solution.py
+++ b/solution.py
@@ -12,6 +12,9 @@
 C = 256
 HALF = 128
 HEADS = 64
+LAG = 5
+RATE = 4
+AHEAD = 3
 MESH = pl.DeviceIdType.MESH
 F32 = jnp.float32
 BF16 = jnp.bfloat16
@@ -42,8 +45,8 @@
 def kernel(
     seq_n, head_n, heads, tokens,
     q_hbm, k_hbm, v_hbm, lam_hbm, gain_ref,
-    out_ref,
-    q_s, k_s, v_s, lam_s, vt_s, acc_s, lv_s, p_s, send_s, recv_s, sq_s, sqx_s, gcol_s, d_s, g_s,
+    out_ref, scale_ref,
+    q_s, k_s, v_s, lam_s, vt_s, acc_s, lv_s, p_s, send_s, recv_s, sq_s, sqx_s, w_s, qt_s, x_s,
     load_sem, lam_sem, send_sem, recv_sem, sq_send_sem, sq_recv_sem,
 ):
     chunks = tokens // C
@@ -61,6 +64,10 @@
 
     lam_copy = pltpu.make_async_copy(lam_hbm, lam_s, lam_sem)
 
+    for h in range(AHEAD):
+        load(2, h).start()
+        load(1, h).start()
+
     barrier = pltpu.get_barrier_semaphore()
     for b in range(bits):
         pl.semaphore_signal(
@@ -71,11 +78,6 @@
             barrier, inc=1, device_id={"head": lax.rem(me_head + k, head_n)}, device_id_type=MESH
         )
 
-    for h in range(heads):
-        load(2, h).start()
-        load(1, h).start()
-    lam_copy.start()
-
     def state_copy(b, h):
         return pltpu.make_async_remote_copy(
             src_ref=send_s.at[b, h],
@@ -86,14 +88,9 @@
             device_id_type=MESH,
         )
 
-    for h in range(heads):
-        row = jnp.broadcast_to(gain_ref[h : h + 1, :], (E, E))
-        gcol_s[h] = row.T
-
     def states(h):
         load(2, h).wait()
         load(1, h).wait()
-        load(0, h).start()
         parts = []
         for c in range(chunks):
             rows = pl.ds(c * C, C)
@@ -113,6 +110,8 @@
         p_s[h] = total.astype(F32)
 
     states(0)
+    load(2, AHEAD).start()
+    load(1, AHEAD).start()
     pl.semaphore_wait(barrier, bits + head_n - 1)
     state_copy(0, 0).start()
 
@@ -121,6 +120,24 @@
         states(h)
         state_copy(0, h).start()
 
+        @pl.when(h + AHEAD < heads)
+        def _():
+            load(2, h + AHEAD).start()
+            load(1, h + AHEAD).start()
+
+        @pl.when(h + AHEAD == heads)
+        def _():
+            load(0, 0).start()
+            lam_copy.start()
+
+        @pl.when(h + AHEAD > heads)
+        def _():
+            load(0, h + AHEAD - heads).start()
+
+    for h in range(AHEAD, heads):
+        load(0, h).start()
+    for c in range(chunks):
+        w_s[c, HALF:C, :HALF] = jnp.zeros((HALF, HALF), BF16)
     lam_copy.wait()
     for h in range(heads):
         lam_s[h] = lam_s[h] * scaling
@@ -154,35 +171,38 @@
                 pieces.append(jnp.where(high == 8 * half + r, fine, spread))
         return jnp.concatenate(pieces, axis=0)
 
-    def inside(h):
-        load(0, h).wait()
-        for c in range(chunks):
-            rows = pl.ds(c * C, C)
-            q = q_s[h, rows, :]
-            lhs = [k_s[h, rows, :]]
-            levels = []
-            for bit in range(chunks.bit_length() - 1):
-                if c >> bit & 1:
-                    start = (c >> bit ^ 1) << bit
-                    lhs.append(lv_s[h, table[(bit, start)]])
-                    levels.append(9 + bit)
-            prod = nt(jnp.concatenate(lhs, axis=0), q)
-            f0 = factors(h, c * C)
-            f1 = factors(h, c * C + HALF)
-            l8 = lam_s[h, pl.ds(8, 1), pl.ds(c * C + HALF, HALF)]
-            top = jnp.concatenate(
-                [(prod[:HALF, :HALF] * f0).astype(BF16), (prod[:HALF, HALF:] * l8).astype(BF16)],
-                axis=1,
-            )
-            bottom = jnp.concatenate(
-                [jnp.zeros((HALF, HALF), BF16), (prod[HALF:C, HALF:] * f1).astype(BF16)], axis=1
-            )
-            weighted = jnp.concatenate([top, bottom], axis=0)
-            acc = nn(vt_s[h, :, rows], weighted)
-            for i, level in enumerate(levels):
-                weight = lam_s[h, pl.ds(level, 1), rows]
-                acc = acc + prod[C + i * E : C + (i + 1) * E] * weight
-            acc_s[h, :, rows] = acc
+    def levels_of(c):
+        found = []
+        for bit in range(chunks.bit_length() - 1):
+            if c >> bit & 1:
+                found.append((9 + bit, table[(bit, (c >> bit ^ 1) << bit)]))
+        return found
+
+    def turn(h, c):
+        rows = pl.ds(c * C, C)
+        qt = q_s[h, rows, :].T
+        qt_s[h, :, rows] = qt
+        wide = qt.astype(F32)
+        for i, (level, _) in enumerate(levels_of(c)):
+            scaled = (wide * lam_s[h, pl.ds(level, 1), rows]).astype(BF16)
+            w_s[c, pl.ds(C + i * D, D), :] = scaled
+
+    def score(h, c):
+        rows = pl.ds(c * C, C)
+        prod = nn(k_s[h, rows, :], qt_s[h, :, rows])
+        f0 = factors(h, c * C)
+        l8 = lam_s[h, pl.ds(8, 1), pl.ds(c * C + HALF, HALF)]
+        at = c
+        w_s[at, :HALF, :HALF] = (prod[:HALF, :HALF] * f0).astype(BF16)
+        w_s[at, :HALF, HALF:] = (prod[:HALF, HALF:] * l8).astype(BF16)
+        f1 = factors(h, c * C + HALF)
+        w_s[at, HALF:C, HALF:] = (prod[HALF:, HALF:] * f1).astype(BF16)
+
+    def gather(h, c):
+        rows = pl.ds(c * C, C)
+        lhs = [vt_s[h, :, rows]] + [lv_s[h, slot] for _, slot in levels_of(c)]
+        depth = C + D * (len(lhs) - 1)
+        acc_s[h, :, rows] = nn(jnp.concatenate(lhs, axis=1), w_s[c, :depth, :])
 
     def relay(b, h):
         copy = state_copy(b, h)
@@ -193,63 +213,68 @@
             send_s[b + 1, h] = total.astype(BF16)
             state_copy(b + 1, h).start()
 
-    LAG = 2
-
-    def relays(slot):
+    def tick(u):
         for b in range(bits):
-            h = slot - b * LAG
+            h = u - b * LAG
 
             @pl.when(jnp.logical_and(h >= 0, h < heads))
             def _():
                 relay(b, h)
 
+    def due(step):
+        return step * RATE // 3
+
     sq_s[...] = jnp.zeros_like(sq_s)
 
     @pl.loop(0, heads)
     def _(h):
-        relays(h)
-        inside(h)
+        pl.loop(due(jnp.maximum(h - 1, 0)), due(h))(tick)
+        load(0, h).wait()
+        for c in range(chunks):
+            turn(h, c)
+        for c in range(chunks):
+            score(h, c)
+        for c in range(chunks):
+            gather(h, c)
 
     on = [(lax.shift_right_logical(me_seq, b) & 1).astype(F32) for b in range(bits)]
 
     def across(h):
-        pieces = 2
-        step = E // pieces
-        for c in range(chunks):
+        cols = pl.ds(pl.multiple_of(h * E, E), E)
+        def spread(c):
             rows = pl.ds(c * C, C)
-            q = q_s[h, rows, :]
-            weights = [lam_s[h, pl.ds(local_bits + 1 + b, 1), rows] * on[b] for b in range(bits)]
+            wide = qt_s[h, :, rows].astype(F32)
+            for b in range(bits):
+                weight = lam_s[h, pl.ds(local_bits + 1 + b, 1), rows] * on[b]
+                x_s[c, pl.ds(b * D, D), :] = (wide * weight).astype(BF16)
+
+        def read(c):
+            rows = pl.ds(c * C, C)
+            lhs = jnp.concatenate([recv_s[h, b] for b in range(bits)], axis=1)
+            acc = acc_s[h, :, rows] + nn(lhs, x_s[c])
+            out_ref[rows, cols] = acc.T * gain_ref[pl.ds(h, 1), :]
+            sq = acc * acc
             square = sq_s[:, rows]
-            lhs = [
-                recv_s[h, b, pl.ds(p * step, step), :] for p in range(pieces) for b in range(bits)
-            ]
-            prod = nt(jnp.concatenate(lhs, axis=0), q)
-            for p in range(pieces):
-                acc = acc_s[h, pl.ds(p * step, step), rows]
-                for b in range(bits):
-                    at = (p * bits + b) * step
-                    acc = acc + prod[at : at + step] * weights[b]
-                acc_s[h, pl.ds(p * step, step), rows] = acc
-                sq = acc * acc
-                for r in range(step // 8):
-                    square = square + sq[r * 8 : (r + 1) * 8]
+            for r in range(E // 8):
+                square = square + sq[r * 8 : (r + 1) * 8]
             sq_s[:, rows] = square
 
-    @pl.loop(0, heads)
-    def _(h):
-        slot = h + heads
-        relays(slot)
-
-        @pl.when(h >= (bits - 1) * LAG)
+        for c in range(chunks):
+            spread(c)
+        for c in range(chunks):
+            read(c)
+
+    last = (bits - 1) * LAG
+
+    @pl.loop(min(due(heads - 1), last), heads + last)
+    def _(u):
+        @pl.when(u >= due(heads - 1))
         def _():
-            across(h - (bits - 1) * LAG)
-
-    first = heads - (bits - 1) * LAG
-
-    @pl.loop(max(first, 0), heads)
-    def _(h):
-        relays(h + heads + (bits - 1) * LAG)
-        across(h)
+            tick(u)
+
+        @pl.when(u >= last)
+        def _():
+            across(u - last)
 
     sqx_s[me_head] = jnp.sum(sq_s[...], axis=0, keepdims=True)
 
@@ -276,27 +301,44 @@
 
     for k in range(1, head_n):
         sq_copy(k).start()
+
+    @pl.loop(0, heads)
+    def _(h):
+        for b in range(bits):
+            state_copy(b, h).wait_send()
+
     for k in range(1, head_n):
         sq_arrive(k).wait_recv()
     total = sqx_s[0]
     for k in range(1, head_n):
         total = total + sqx_s[k]
-    scale = lax.rsqrt(total / (HEADS * E) + 1e-05)
-    sqx_s[head_n] = scale
-
-    @pl.loop(0, heads)
-    def _(h):
-        cols = pl.ds(pl.multiple_of(h * E, E), E)
-        for c in range(tokens // HALF):
-            rows = pl.ds(c * HALF, HALF)
-            value = acc_s[h, :, rows] * gcol_s[h] * sqx_s[head_n, :, rows]
-            out_ref[rows, cols] = value.astype(BF16).T
-
-    for b in range(bits):
-        for h in range(heads):
-            state_copy(b, h).wait_send()
+    scale_ref[...] = lax.rsqrt(total / (HEADS * E) + 1e-05)
+
     for k in range(1, head_n):
         sq_copy(k).wait_send()
+
+
+def finish(tokens, acc_ref, scale_ref, out_hbm, buf, col_s, sem):
+    def out_copy(i):
+        rows = pl.ds(i * HALF, HALF)
+        return pltpu.make_async_copy(buf.at[i], out_hbm.at[rows, :], sem.at[i])
+
+    def turn(i):
+        rows = pl.ds(i * HALF, HALF)
+        col_s[rows, :] = jnp.broadcast_to(scale_ref[:, rows], (HALF, HALF)).T
+
+    blocks = tokens // HALF
+    turn(0)
+    for i in range(blocks):
+        if i + 1 < blocks:
+            turn(i + 1)
+        rows = pl.ds(i * HALF, HALF)
+        for h in range(acc_ref.shape[1] // E):
+            cols = pl.ds(h * E, E)
+            buf[i, :, cols] = (acc_ref[rows, cols] * col_s[rows, :]).astype(BF16)
+        out_copy(i).start()
+    for i in range(blocks):
+        out_copy(i).wait()
 
 
 def body(queries, key_vectors, value_vectors, level_weights, norm_gain):
@@ -308,11 +350,11 @@
     slots = max(len(buckets_of(tokens // C)), 1)
     any_spec = pl.BlockSpec(memory_space=pl.ANY)
     vmem = pl.BlockSpec(memory_space=pltpu.VMEM)
-    return pl.pallas_call(
+    mixture, scale = pl.pallas_call(
         functools.partial(kernel, seq_n, head_n, heads, tokens),
-        out_shape=jax.ShapeDtypeStruct((tokens, heads * E), BF16),
-        in_specs=[any_spec] * 4 + [vmem],
-        out_specs=vmem,
+        out_shape=(pltpu.VMEM((tokens, heads * E), F32), pltpu.VMEM((1, tokens), F32)),
+        in_specs=[pl.BlockSpec(memory_space=pltpu.HBM)] * 4 + [vmem],
+        out_specs=(vmem, vmem),
         scratch_shapes=[
             pltpu.VMEM((heads, tokens, D), BF16),
             pltpu.VMEM((heads, tokens, D), BF16),
@@ -325,10 +367,10 @@
             pltpu.VMEM((bits, heads, E, D), BF16),
             pltpu.VMEM((heads, bits, E, D), BF16),
             pltpu.VMEM((8, tokens), F32),
-            pltpu.VMEM((head_n + 1, 1, tokens), F32),
-            pltpu.VMEM((heads, E, E), F32),
-            pltpu.VMEM((8, HALF), F32),
-            pltpu.VMEM((16, HALF), F32),
+            pltpu.VMEM((head_n, 1, tokens), F32),
+            pltpu.VMEM((tokens // C, C + 3 * D, C), BF16),
+            pltpu.VMEM((heads, D, tokens), BF16),
+            pltpu.VMEM((tokens // C, bits * D, C), BF16),
             pltpu.SemaphoreType.DMA((3, heads)),
             pltpu.SemaphoreType.DMA,
             pltpu.SemaphoreType.DMA((bits, heads)),
@@ -337,10 +379,23 @@
             pltpu.SemaphoreType.DMA((head_n,)),
         ],
         compiler_params=pltpu.CompilerParams(
-            collective_id=0, has_side_effects=True, vmem_limit_bytes=60 * 1024 * 1024
+            collective_id=0, has_side_effects=True, vmem_limit_bytes=58 * 1000 * 1000
         ),
         name="fenwick",
     )(queries, key_vectors, value_vectors, level_weights, norm_gain.reshape(heads, E))
+    return pl.pallas_call(
+        functools.partial(finish, tokens),
+        out_shape=jax.ShapeDtypeStruct((tokens, heads * E), BF16),
+        in_specs=[vmem, vmem],
+        out_specs=any_spec,
+        scratch_shapes=[
+            pltpu.VMEM((tokens // HALF, HALF, heads * E), BF16),
+            pltpu.VMEM((tokens, HALF), F32),
+            pltpu.SemaphoreType.DMA((tokens // HALF,)),
+        ],
+        compiler_params=pltpu.CompilerParams(vmem_limit_bytes=16 * 1024 * 1024),
+        name="finish",
+    )(mixture, scale)
 
 
 def solution(mesh):

time: 52.8 us -> 36.9 us (0.70)
  Pallas kernels: 48 us -> 36.7 us
  local copies, waits for them, and re-layouts: 4.64 us -> 0 us
    pallas_call x1, Pallas kernels: 48 us -> 34.4 us  [body(): pl.pallas_call(functools.partial(kernel, seq_n, head_n, heads, tokens), o...]
    unnamed x1 -> x0, local copies, waits for them, and re-layouts: 4.64 us -> none
    pallas_call x0 -> x1, Pallas kernels: none -> 2.27 us  [body(): pl.pallas_call(functools.partial(finish, tokens), out_shape=jax.ShapeDtyp...]
where the time goes in v1:
time: 36.9 us; the launch traced here: 36.7 us
  Pallas kernels  36.7 us (99%)
    pallas_call x1, Pallas kernels, body(): pl.pallas_call(functools.partial(kernel, seq_n, head_n, heads, tokens), o...  34.4 us
    pallas_call x1, Pallas kernels, body(): pl.pallas_call(functools.partial(finish, tokens), out_shape=jax.ShapeDtyp...  2.27 us

profile of v1, /device:TPU:1, one launch (start us, length us, event | category | flops | bytes accessed | tf_op | source)
XLA Modules:
  0.0 36.7 jit_solution(13359749517515360666)
XLA Ops:
  0.0 34.4 %fenwick.1 = (f32[2048,1024]{1,0:T(8,128)S(1)}, f32[1,2048]{1,0:T(1,128)S(1)}) custom-call(bf16[2048,1024]{1,0:T(8,128)(2,1)} %q_hbm.1, bf16[2048,1024]{1,0:T(8,128)(2,1)} %k_hbm.1, bf16[2048,1024]{1,0:T(8,128)(2,1)} %v_hbm.1, f32[8,16,2048]{2,1,0:T(8,128)} %lam_hbm.1, f32[8,128]{1,0:T(8,128)} %bitcast.1), custom_call_target="tpu_custom_call" | custom-call | tf_op jit(solution)/shard_map/fenwick/pallas_call | solution.py:353
  34.4 2.3 %finish.1 = bf16[2048,1024]{1,0:T(8,128)(2,1)} custom-call(f32[2048,1024]{1,0:T(8,128)S(1)} %get-tuple-element.7.acc_ref, f32[1,2048]{1,0:T(1,128)S(1)} %get-tuple-element.8.scale_ref), custom_call_target="tpu_custom_call" | custom-call | tf_op jit(solution)/shard_map/finish/pallas_call | solution.py:386

commit v2 on v1

--- a/solution.py
+++ b/solution.py
@@ -12,7 +12,7 @@
 C = 256
 HALF = 128
 HEADS = 64
-LAG = 5
+LAG = 4
 RATE = 4
 AHEAD = 3
 MESH = pl.DeviceIdType.MESH
@@ -30,6 +30,12 @@
 
 def partner_mask(bit):
     return 1 << bit if bit % 2 == 0 else 3 << (bit - 1)
+
+
+def scaled(qt, row):
+    width = qt.shape[1]
+    weight = jnp.broadcast_to(row, (16, width)).astype(BF16)
+    return qt * jnp.concatenate([weight] * (qt.shape[0] // 16), axis=0)
 
 
 def buckets_of(chunks):
@@ -87,6 +93,14 @@
             device_id={"seq": me_seq ^ partner_mask(b)},
             device_id_type=MESH,
         )
+
+    sends = [me_seq < seq_n - (1 << b) for b in range(bits)]
+    gets = [(me_seq ^ partner_mask(b)) < seq_n - (1 << b) for b in range(bits)]
+
+    def send_state(b, h):
+        @pl.when(sends[b])
+        def _():
+            state_copy(b, h).start()
 
     def states(h):
         load(2, h).wait()
@@ -113,12 +127,12 @@
     load(2, AHEAD).start()
     load(1, AHEAD).start()
     pl.semaphore_wait(barrier, bits + head_n - 1)
-    state_copy(0, 0).start()
+    send_state(0, 0)
 
     @pl.loop(1, heads)
     def _(h):
         states(h)
-        state_copy(0, h).start()
+        send_state(0, h)
 
         @pl.when(h + AHEAD < heads)
         def _():
@@ -182,10 +196,8 @@
         rows = pl.ds(c * C, C)
         qt = q_s[h, rows, :].T
         qt_s[h, :, rows] = qt
-        wide = qt.astype(F32)
         for i, (level, _) in enumerate(levels_of(c)):
-            scaled = (wide * lam_s[h, pl.ds(level, 1), rows]).astype(BF16)
-            w_s[c, pl.ds(C + i * D, D), :] = scaled
+            w_s[c, pl.ds(C + i * D, D), :] = scaled(qt, lam_s[h, pl.ds(level, 1), rows])
 
     def score(h, c):
         rows = pl.ds(c * C, C)
@@ -205,13 +217,16 @@
         acc_s[h, :, rows] = nn(jnp.concatenate(lhs, axis=1), w_s[c, :depth, :])
 
     def relay(b, h):
-        copy = state_copy(b, h)
-        copy.wait_recv()
-        if b + 1 < bits:
-            total = p_s[h] + recv_s[h, b].astype(F32)
-            p_s[h] = total
-            send_s[b + 1, h] = total.astype(BF16)
-            state_copy(b + 1, h).start()
+        @pl.when(gets[b])
+        def _():
+            state_copy(b, h).wait_recv()
+            if b + 1 < bits:
+                @pl.when(sends[b + 1])
+                def _():
+                    total = p_s[h] + recv_s[h, b].astype(F32)
+                    p_s[h] = total
+                    send_s[b + 1, h] = total.astype(BF16)
+                    state_copy(b + 1, h).start()
 
     def tick(u):
         for b in range(bits):
@@ -225,6 +240,12 @@
         return step * RATE // 3
 
     sq_s[...] = jnp.zeros_like(sq_s)
+    for b in range(bits):
+        @pl.when(jnp.logical_not(gets[b]))
+        def _():
+            for h in range(heads):
+                recv_s[h, b] = jnp.zeros((E, D), BF16)
+
 
     @pl.loop(0, heads)
     def _(h):
@@ -243,10 +264,10 @@
         cols = pl.ds(pl.multiple_of(h * E, E), E)
         def spread(c):
             rows = pl.ds(c * C, C)
-            wide = qt_s[h, :, rows].astype(F32)
+            qt = qt_s[h, :, rows]
             for b in range(bits):
                 weight = lam_s[h, pl.ds(local_bits + 1 + b, 1), rows] * on[b]
-                x_s[c, pl.ds(b * D, D), :] = (wide * weight).astype(BF16)
+                x_s[c, pl.ds(b * D, D), :] = scaled(qt, weight)
 
         def read(c):
             rows = pl.ds(c * C, C)
@@ -299,13 +320,15 @@
             device_id_type=MESH,
         )
 
-    for k in range(1, head_n):
+    for k in sorted(range(1, head_n), key=lambda k: abs(k - head_n // 2)):
         sq_copy(k).start()
 
     @pl.loop(0, heads)
     def _(h):
         for b in range(bits):
-            state_copy(b, h).wait_send()
+            @pl.when(sends[b])
+            def _():
+                state_copy(b, h).wait_send()
 
     for k in range(1, head_n):
         sq_arrive(k).wait_recv()

time: 36.9 us -> 34.7 us (0.940)
  Pallas kernels: 36.7 us -> 34.5 us
    pallas_call x1, Pallas kernels: 34.4 us -> 32.2 us  [body(): pl.pallas_call(functools.partial(kernel, seq_n, head_n, heads, tokens), o...]
where the time goes in v2:
time: 34.7 us; the launch traced here: 34.5 us
  Pallas kernels  34.5 us (99%)
    pallas_call x1, Pallas kernels, body(): pl.pallas_call(functools.partial(kernel, seq_n, head_n, heads, tokens), o...  32.2 us
    pallas_call x1, Pallas kernels, body(): pl.pallas_call(functools.partial(finish, tokens), out_shape=jax.ShapeDtyp...  2.27 us

profile of v2, /device:TPU:1, one launch (start us, length us, event | category | flops | bytes accessed | tf_op | source)
XLA Modules:
  0.0 34.5 jit_solution(5293436027653525053)
XLA Ops:
  0.0 32.2 %fenwick.1 = (f32[2048,1024]{1,0:T(8,128)S(1)}, f32[1,2048]{1,0:T(1,128)S(1)}) custom-call(bf16[2048,1024]{1,0:T(8,128)(2,1)} %q_hbm.1, bf16[2048,1024]{1,0:T(8,128)(2,1)} %k_hbm.1, bf16[2048,1024]{1,0:T(8,128)(2,1)} %v_hbm.1, f32[8,16,2048]{2,1,0:T(8,128)} %lam_hbm.1, f32[8,128]{1,0:T(8,128)} %bitcast.1), custom_call_target="tpu_custom_call" | custom-call | tf_op jit(solution)/shard_map/fenwick/pallas_call | solution.py:376
  32.2 2.3 %finish.1 = bf16[2048,1024]{1,0:T(8,128)(2,1)} custom-call(f32[2048,1024]{1,0:T(8,128)S(1)} %get-tuple-element.7.acc_ref, f32[1,2048]{1,0:T(1,128)S(1)} %get-tuple-element.8.scale_ref), custom_call_target="tpu_custom_call" | custom-call | tf_op jit(solution)/shard_map/finish/pallas_call | solution.py:409

commit v3 on v2

--- a/solution.py
+++ b/solution.py
@@ -14,7 +14,7 @@
 HEADS = 64
 LAG = 4
 RATE = 4
-AHEAD = 3
+AHEAD = 8
 MESH = pl.DeviceIdType.MESH
 F32 = jnp.float32
 BF16 = jnp.bfloat16
@@ -70,18 +70,19 @@
 
     lam_copy = pltpu.make_async_copy(lam_hbm, lam_s, lam_sem)
 
+    barrier = pltpu.get_barrier_semaphore()
+    for k in sorted(range(1, head_n), key=lambda k: abs(k - head_n // 2)):
+        pl.semaphore_signal(
+            barrier, inc=1, device_id={"head": lax.rem(me_head + k, head_n)}, device_id_type=MESH
+        )
+
     for h in range(AHEAD):
         load(2, h).start()
         load(1, h).start()
 
-    barrier = pltpu.get_barrier_semaphore()
     for b in range(bits):
         pl.semaphore_signal(
             barrier, inc=1, device_id={"seq": me_seq ^ partner_mask(b)}, device_id_type=MESH
-        )
-    for k in range(1, head_n):
-        pl.semaphore_signal(
-            barrier, inc=1, device_id={"head": lax.rem(me_head + k, head_n)}, device_id_type=MESH
         )
 
     def state_copy(b, h):
@@ -124,8 +125,8 @@
         p_s[h] = total.astype(F32)
 
     states(0)
-    load(2, AHEAD).start()
-    load(1, AHEAD).start()
+    load(0, 0).start()
+    lam_copy.start()
     pl.semaphore_wait(barrier, bits + head_n - 1)
     send_state(0, 0)
 
@@ -134,19 +135,7 @@
         states(h)
         send_state(0, h)
 
-        @pl.when(h + AHEAD < heads)
-        def _():
-            load(2, h + AHEAD).start()
-            load(1, h + AHEAD).start()
-
-        @pl.when(h + AHEAD == heads)
-        def _():
-            load(0, 0).start()
-            lam_copy.start()
-
-        @pl.when(h + AHEAD > heads)
-        def _():
-            load(0, h + AHEAD - heads).start()
+        load(0, h).start()
 
     for h in range(AHEAD, heads):
         load(0, h).start()
@@ -261,7 +250,6 @@
     on = [(lax.shift_right_logical(me_seq, b) & 1).astype(F32) for b in range(bits)]
 
     def across(h):
-        cols = pl.ds(pl.multiple_of(h * E, E), E)
         def spread(c):
             rows = pl.ds(c * C, C)
             qt = qt_s[h, :, rows]
@@ -273,7 +261,7 @@
             rows = pl.ds(c * C, C)
             lhs = jnp.concatenate([recv_s[h, b] for b in range(bits)], axis=1)
             acc = acc_s[h, :, rows] + nn(lhs, x_s[c])
-            out_ref[rows, cols] = acc.T * gain_ref[pl.ds(h, 1), :]
+            acc_s[h, :, rows] = acc
             sq = acc * acc
             square = sq_s[:, rows]
             for r in range(E // 8):
@@ -322,6 +310,13 @@
 
     for k in sorted(range(1, head_n), key=lambda k: abs(k - head_n // 2)):
         sq_copy(k).start()
+
+    @pl.loop(0, heads)
+    def _(h):
+        cols = pl.ds(pl.multiple_of(h * E, E), E)
+        for c in range(chunks):
+            rows = pl.ds(c * C, C)
+            out_ref[rows, cols] = acc_s[h, :, rows].T * gain_ref[pl.ds(h, 1), :]
 
     @pl.loop(0, heads)
     def _(h):

time: 34.7 us -> 32.6 us (0.939)
  Pallas kernels: 34.5 us -> 32.5 us
    pallas_call x1, Pallas kernels: 32.2 us -> 30.2 us  [body(): pl.pallas_call(functools.partial(kernel, seq_n, head_n, heads, tokens), o...]
where the time goes in v3:
time: 32.6 us; the launch traced here: 32.5 us
  Pallas kernels  32.5 us (100%)
    pallas_call x1, Pallas kernels, body(): pl.pallas_call(functools.partial(kernel, seq_n, head_n, heads, tokens), o...  30.2 us
    pallas_call x1, Pallas kernels, body(): pl.pallas_call(functools.partial(finish, tokens), out_shape=jax.ShapeDtyp...  2.27 us

profile of v3, /device:TPU:1, one launch (start us, length us, event | category | flops | bytes accessed | tf_op | source)
XLA Modules:
  0.0 32.5 jit_solution(863053166969905235)
XLA Ops:
  0.0 30.2 %fenwick.1 = (f32[2048,1024]{1,0:T(8,128)S(1)}, f32[1,2048]{1,0:T(1,128)S(1)}) custom-call(bf16[2048,1024]{1,0:T(8,128)(2,1)} %q_hbm.1, bf16[2048,1024]{1,0:T(8,128)(2,1)} %k_hbm.1, bf16[2048,1024]{1,0:T(8,128)(2,1)} %v_hbm.1, f32[8,16,2048]{2,1,0:T(8,128)} %lam_hbm.1, f32[8,128]{1,0:T(8,128)} %bitcast.1), custom_call_target="tpu_custom_call" | custom-call | tf_op jit(solution)/shard_map/fenwick/pallas_call | solution.py:371
  30.2 2.3 %finish.1 = bf16[2048,1024]{1,0:T(8,128)(2,1)} custom-call(f32[2048,1024]{1,0:T(8,128)S(1)} %get-tuple-element.7.acc_ref, f32[1,2048]{1,0:T(1,128)S(1)} %get-tuple-element.8.scale_ref), custom_call_target="tpu_custom_call" | custom-call | tf_op jit(solution)/shard_map/finish/pallas_call | solution.py:404

commit v4 on v3

--- a/solution.py
+++ b/solution.py
@@ -226,7 +226,7 @@
                 relay(b, h)
 
     def due(step):
-        return step * RATE // 3
+        return (step * RATE + 2) // 3
 
     sq_s[...] = jnp.zeros_like(sq_s)
     for b in range(bits):

time: 32.6 us -> 32.4 us (level)
  no operation moved by 1% of the time
where the time goes in v4:
time: 32.4 us; the launch traced here: 32.3 us
  Pallas kernels  32.3 us (100%)
    pallas_call x1, Pallas kernels, body(): pl.pallas_call(functools.partial(kernel, seq_n, head_n, heads, tokens), o...  30 us
    pallas_call x1, Pallas kernels, body(): pl.pallas_call(functools.partial(finish, tokens), out_shape=jax.ShapeDtyp...  2.27 us

profile of v4, /device:TPU:1, one launch (start us, length us, event | category | flops | bytes accessed | tf_op | source)
XLA Modules:
  0.0 32.3 jit_solution(15850357458766219089)
XLA Ops:
  0.0 30.0 %fenwick.1 = (f32[2048,1024]{1,0:T(8,128)S(1)}, f32[1,2048]{1,0:T(1,128)S(1)}) custom-call(bf16[2048,1024]{1,0:T(8,128)(2,1)} %q_hbm.1, bf16[2048,1024]{1,0:T(8,128)(2,1)} %k_hbm.1, bf16[2048,1024]{1,0:T(8,128)(2,1)} %v_hbm.1, f32[8,16,2048]{2,1,0:T(8,128)} %lam_hbm.1, f32[8,128]{1,0:T(8,128)} %bitcast.1), custom_call_target="tpu_custom_call" | custom-call | tf_op jit(solution)/shard_map/fenwick/pallas_call | solution.py:371
  30.0 2.3 %finish.1 = bf16[2048,1024]{1,0:T(8,128)(2,1)} custom-call(f32[2048,1024]{1,0:T(8,128)S(1)} %get-tuple-element.7.acc_ref, f32[1,2048]{1,0:T(1,128)S(1)} %get-tuple-element.8.scale_ref), custom_call_target="tpu_custom_call" | custom-call | tf_op jit(solution)/shard_map/finish/pallas_call | solution.py:404
